TPU v7x, 32 devices: a whole 2x2x4 slice. The times are simulated.
32 devices in a mesh: lat: 8 (over y, x, core), lon: 4 (over z).
Axes of the slice: x: 2, y: 2, z: 4, core: 2. Of those that a mesh axis runs over, the one named last changes fastest.
Arguments:
- snapshots: float32 [1024, 128, 512], P(None, 'lat', 'lon'), may hold values from -60 to 60
- land_sea: int32 [128, 512], P('lat', 'lon'), may hold values 0 or 1
- penalty: float32 [128, 512], P('lat', 'lon'), may hold values from 0.003 to 0.03
- initial_basis: float32 [64, 128, 512], P(None, 'lat', 'lon'), may hold values from -6 to 6
Outputs:
- leading_basis: float32 [64, 128, 512], P(None, 'lat', 'lon')
- rayleigh_matrix: float32 [64, 64], replicated
All inputs are finite; a program needn't handle non-finite values. No bound on the sum of `land_sea` on one device may be relied on, other than what follows from the above.
Results may differ from a plain program's by a relative error of at most 0.0003.
Values sent between devices are 32-bit elements; how exact they have to be, the bound alone decides.
A program may use at most 64 MiB of HBM per device.

v0:
```python
import jax
import jax.numpy as jnp
from jax import lax
from jax.sharding import PartitionSpec as P

STEPS = 2


def padded_2(block, sides, width):
    for axis, dim in sides:
        count = lax.axis_size(axis)
        forward = [(i, i + 1) for i in range(count - 1)]
        backward = [(target, source) for source, target in forward]
        low = lax.ppermute(
            lax.slice_in_dim(block, block.shape[dim] - width, None, axis=dim), axis, forward
        )
        high = lax.ppermute(lax.slice_in_dim(block, 0, width, axis=dim), axis, backward)
        block = jnp.concatenate([low, block, high], axis=dim)
    return block


def laplacian(masked_field):
    padded = padded_2(masked_field, (("lat", 1), ("lon", 2)), 1)
    neighbours = (
        padded[:, 2:, 1:-1] + padded[:, :-2, 1:-1] + padded[:, 1:-1, 2:] + padded[:, 1:-1, :-2]
    )
    return neighbours - 4.0 * masked_field


def project_points(snapshots, masked_field):
    return jnp.einsum("tab,kab->tk", snapshots, masked_field, precision=lax.Precision.HIGHEST)


def expand_points(snapshots, coeffs):
    return jnp.einsum("tab,tk->kab", snapshots, coeffs, precision=lax.Precision.HIGHEST)


def inner_products(left_field, right_field):
    return jnp.einsum("kab,jab->kj", left_field, right_field, precision=lax.Precision.HIGHEST)


def apply_inverse(factor, stacked):
    solved = jax.scipy.linalg.solve_triangular(
        factor, stacked.reshape(stacked.shape[0], -1), lower=True
    )
    return solved.reshape(stacked.shape)


def total_terms(term_tuple):
    shares = (lax.psum_scatter(term_tuple[0], "lat", scatter_dimension=0, tiled=True),)
    summed = lax.psum((shares[0],), "lon")
    return (lax.all_gather(summed[0], "lat", axis=0, tiled=True),)


def local(snapshots, land_sea, penalty, initial_basis):
    ocean_mask = land_sea.astype(jnp.float32)
    point_count = float(
        snapshots.shape[1] * snapshots.shape[2] * lax.axis_size("lat") * lax.axis_size("lon")
    )
    current_basis = initial_basis * ocean_mask
    for iteration in range(STEPS):
        (coeffs,) = total_terms((project_points(snapshots, current_basis),))
        applied = ocean_mask * (
            expand_points(snapshots, coeffs) / point_count + penalty * laplacian(current_basis)
        )
        (moments,) = total_terms((inner_products(applied, applied),))
        factor = jnp.linalg.cholesky(moments / point_count)
        current_basis = apply_inverse(factor, applied)
    (coeffs,) = total_terms((project_points(snapshots, current_basis),))
    smoothed = laplacian(current_basis)
    final_image = ocean_mask * (expand_points(snapshots, coeffs) / point_count + penalty * smoothed)
    (projected,) = total_terms((inner_products(current_basis, final_image),))
    return (current_basis, projected / point_count)


def solution(mesh):
    in_specs = (P(None, "lat", "lon"), P("lat", "lon"), P("lat", "lon"), P(None, "lat", "lon"))
    out_specs = (P(None, "lat", "lon"), P())
    return jax.shard_map(local, mesh=mesh, in_specs=in_specs, out_specs=out_specs, check_vma=False)
```

profile of v0, /device:TPU:0, one launch (start us, length us, event | category | flops | bytes accessed | tf_op | source)
XLA Modules:
  0.0 464.0 jit_solution(17767832957010539441)
XLA Ops:
  13.5 12.8 %fusion.39 = f32[1024,64]{0,1:T(8,128)} fusion(f32[64,16,128]{2,0,1:T(8,128)S(1)} %copy_multiply_fusion, f32[1024,16,128]{2,1,0:T(8,128)} %param.7), kind=kOutput, calls=%fused_computation.22 | convolution fusion | flops 1610612736 | bytes 9175040 | tf_op jit(solution)/shard_map/tab,kab->tk/dot_general | solution.py:31
  35.9 27.7 %reduce-scatter.7.cloned.1.call-done = f32[128,64]{0,1:T(8,128)} async-done(((f32[1024,64]{0,1:T(8,128)}), f32[128,64]{0,1:T(8,128)}) %reduce-scatter.7.cloned.1.call-update) | async-done | bytes 32784 | tf_op jit(solution)/shard_map/reduce_scatter | solution.py:50
  63.6 19.6 %psum.42 = f32[128,64]{0,1:T(8,128)S(1)} all-reduce(f32[128,64]{0,1:T(8,128)} %reduce-scatter.7.cloned.1.call-done), channel_id=1, replica_groups=mesh['lat'=8,'lon'=4] {'lon'}, use_global_device_ids=true, to_apply=%region_1.0 | all-reduce | flops 8192 | bytes 65536 | tf_op jit(solution)/shard_map/psum | solution.py:51
  83.2 9.8 %all_gather.18 = f32[1024,64]{0,1:T(8,128)S(1)} all-gather(f32[128,64]{0,1:T(8,128)S(1)} %psum.42), channel_id=1, replica_groups=mesh['lat'=8,'lon'=4] {'lat'}, dimensions={0}, use_global_device_ids=true | all-gather | bytes 294912 | tf_op jit(solution)/shard_map/all_gather | solution.py:52
  93.0 9.8 %fusion.36 = f32[64,16,128]{2,0,1:T(8,128)S(1)} fusion(f32[1024,16,128]{2,1,0:T(8,128)} %param.7, f32[64,18,1]{2,0,1:T(8,128)S(1)} %copy.46, f32[64,1,128]{2,0,1:T(8,128)S(1)} %collective-permute-done, f32[64,16,128]{2,0,1:T(8,128)S(1)} %copy_multiply_fusion, f32[64,1,128]{2,0,1:T(8,128)S(1)} %collective-permute-done.1, f32[64,18,1]{2,0,1:T(8,128)S(1)} %copy.44, ...), kind=kOutput, calls=%fused_computation.20 | convolution fusion | flops 1612840960 | bytes 9790464 | tf_op jit(solution)/shard_map/tab,tk->kab/dot_general | solution.py:35
  103.4 23.6 %all-reduce = f32[64,64]{0,1:T(8,128)S(1)} all-reduce(f32[64,64]{0,1:T(8,128)S(1)} %convolution_bitcast_fusion.3), channel_id=3, replica_groups=mesh['lat'=8,'lon'=4] {'lat'}, use_global_device_ids=true, to_apply=%region_2.0.clone | all-reduce | flops 4096 | bytes 32768
  127.0 15.8 %psum.43 = f32[8,64]{0,1:T(8,128)S(1)} all-reduce(f32[8,64]{0,1:T(8,128)S(1)} %constant_dynamic-slice_fusion.2), channel_id=1, replica_groups=mesh['lat'=8,'lon'=4] {'lon'}, use_global_device_ids=true, to_apply=%region_3.0 | all-reduce | flops 512 | bytes 4096 | tf_op jit(solution)/shard_map/psum | solution.py:51
  142.9 8.3 %all_gather.19 = f32[64,64]{1,0:T(8,128)S(1)} all-gather(f32[8,64]{1,0:T(8,128)S(1)} %copy.48), channel_id=1, replica_groups=mesh['lat'=8,'lon'=4] {'lat'}, dimensions={0}, use_global_device_ids=true | all-gather | bytes 18432 | tf_op jit(solution)/shard_map/all_gather | solution.py:52
  166.4 12.8 %fusion.42 = f32[1024,64]{0,1:T(8,128)} fusion(f32[1024,16,128]{2,1,0:T(8,128)} %param.7, f32[8,16,8,128]{3,2,1,0:T(8,128)S(1)} %convolution_bitcast_fusion), kind=kOutput, calls=%fused_computation.23 | convolution fusion | flops 1610612736 | bytes 9175040 | tf_op jit(solution)/shard_map/tab,kab->tk/dot_general | solution.py:31
  191.2 24.7 %reduce-scatter.9.cloned.1.call-done = f32[128,64]{0,1:T(8,128)} async-done(((f32[1024,64]{0,1:T(8,128)}), f32[128,64]{0,1:T(8,128)}) %reduce-scatter.9.cloned.1.call-update) | async-done | bytes 32784 | tf_op jit(solution)/shard_map/reduce_scatter | solution.py:50
  216.0 19.6 %psum.44 = f32[128,64]{0,1:T(8,128)S(1)} all-reduce(f32[128,64]{0,1:T(8,128)} %reduce-scatter.9.cloned.1.call-done), channel_id=1, replica_groups=mesh['lat'=8,'lon'=4] {'lon'}, use_global_device_ids=true, to_apply=%region_7.0 | all-reduce | flops 8192 | bytes 65536 | tf_op jit(solution)/shard_map/psum | solution.py:51
  235.6 10.0 %all_gather.20 = f32[1024,64]{0,1:T(8,128)S(1)} all-gather(f32[128,64]{0,1:T(8,128)S(1)} %psum.44), channel_id=1, replica_groups=mesh['lat'=8,'lon'=4] {'lat'}, dimensions={0}, use_global_device_ids=true | all-gather | bytes 294912 | tf_op jit(solution)/shard_map/all_gather | solution.py:52
  245.6 9.8 %fusion.33 = f32[64,16,128]{2,0,1:T(8,128)S(1)} fusion(f32[1024,16,128]{2,1,0:T(8,128)} %param.7, f32[64,18,128]{2,0,1:T(8,128)S(1)} %constant_dynamic-update-slice_fusion, f32[64,18,1]{2,0,1:T(8,128)S(1)} %copy.63, f32[64,18,1]{2,0,1:T(8,128)S(1)} %copy.61, f32[64,16,128]{2,0,1:T(8,128)S(1)} %bitcast.101, f32[64,1,128]{2,0,1:T(8,128)S(1)} %collective-permute-done.5, ...), kind=kOutput, calls=%fused_computation.19 | convolution fusion | flops 1612316672 | bytes 10380288 | tf_op jit(solution)/shard_map/tab,tk->kab/dot_general | solution.py:35
  256.0 23.6 %all-reduce.1 = f32[64,64]{0,1:T(8,128)S(1)} all-reduce(f32[64,64]{0,1:T(8,128)S(1)} %convolution_bitcast_fusion.2), channel_id=5, replica_groups=mesh['lat'=8,'lon'=4] {'lat'}, use_global_device_ids=true, to_apply=%region_8.0.clone | all-reduce | flops 4096 | bytes 32768
  279.7 15.8 %psum.45 = f32[8,64]{0,1:T(8,128)S(1)} all-reduce(f32[8,64]{0,1:T(8,128)S(1)} %constant_dynamic-slice_fusion.1), channel_id=1, replica_groups=mesh['lat'=8,'lon'=4] {'lon'}, use_global_device_ids=true, to_apply=%region_9.0 | all-reduce | flops 512 | bytes 4096 | tf_op jit(solution)/shard_map/psum | solution.py:51
  295.5 8.1 %all_gather.21 = f32[64,64]{1,0:T(8,128)S(1)} all-gather(f32[8,64]{1,0:T(8,128)S(1)} %copy.66), channel_id=1, replica_groups=mesh['lat'=8,'lon'=4] {'lat'}, dimensions={0}, use_global_device_ids=true | all-gather | bytes 18432 | tf_op jit(solution)/shard_map/all_gather | solution.py:52
  318.9 12.8 %fusion.45 = f32[1024,64]{0,1:T(8,128)} fusion(f32[1024,16,128]{2,1,0:T(8,128)} %param.7, f32[64,2048]{1,0:T(8,128)S(1)} %fusion.48), kind=kOutput, calls=%fused_computation.24 | convolution fusion | flops 1610612736 | bytes 9175040 | tf_op jit(solution)/shard_map/tab,kab->tk/dot_general | solution.py:31
  343.7 25.0 %reduce-scatter.11.cloned.1.call-done = f32[128,64]{0,1:T(8,128)} async-done(((f32[1024,64]{0,1:T(8,128)}), f32[128,64]{0,1:T(8,128)}) %reduce-scatter.11.cloned.1.call-update) | async-done | bytes 32784 | tf_op jit(solution)/shard_map/reduce_scatter | solution.py:50
  368.7 19.6 %psum.46 = f32[128,64]{0,1:T(8,128)S(1)} all-reduce(f32[128,64]{0,1:T(8,128)} %reduce-scatter.11.cloned.1.call-done), channel_id=1, replica_groups=mesh['lat'=8,'lon'=4] {'lon'}, use_global_device_ids=true, to_apply=%region_11.0 | all-reduce | flops 8192 | bytes 65536 | tf_op jit(solution)/shard_map/psum | solution.py:51
  388.3 9.8 %all_gather.22 = f32[1024,64]{0,1:T(8,128)S(1)} all-gather(f32[128,64]{0,1:T(8,128)S(1)} %psum.46), channel_id=1, replica_groups=mesh['lat'=8,'lon'=4] {'lat'}, dimensions={0}, use_global_device_ids=true | all-gather | bytes 294912 | tf_op jit(solution)/shard_map/all_gather | solution.py:52
  398.2 9.8 %fusion.30 = f32[64,16,128]{2,0,1:T(8,128)S(1)} fusion(f32[1024,16,128]{2,1,0:T(8,128)} %param.7, f32[64,18,128]{2,0,1:T(8,128)S(1)} %constant_dynamic-update-slice_fusion.3, f32[64,18,1]{2,0,1:T(8,128)S(1)} %copy.81, f32[64,18,1]{2,0,1:T(8,128)S(1)} %copy.79, f32[64,16,128]{2,0,1:T(8,128)S(1)} %copy_bitcast_fusion, ...), kind=kOutput, calls=%fused_computation.18 | convolution fusion | flops 1612316672 | bytes 10380288 | tf_op jit(solution)/shard_map/tab,tk->kab/dot_general | solution.py:35
  408.6 23.6 %all-reduce.2 = f32[64,64]{0,1:T(8,128)S(1)} all-reduce(f32[64,64]{0,1:T(8,128)S(1)} %convolution_bitcast_fusion.1), channel_id=7, replica_groups=mesh['lat'=8,'lon'=4] {'lat'}, use_global_device_ids=true, to_apply=%region_12.15.clone | all-reduce | flops 4096 | bytes 32768
  432.3 15.8 %psum.47 = f32[8,64]{0,1:T(8,128)S(1)} all-reduce(f32[8,64]{0,1:T(8,128)S(1)} %constant_dynamic-slice_fusion), channel_id=1, replica_groups=mesh['lat'=8,'lon'=4] {'lon'}, use_global_device_ids=true, to_apply=%region_13.16 | all-reduce | flops 512 | bytes 4096 | tf_op jit(solution)/shard_map/psum | solution.py:51
  448.1 8.2 %all_gather.23 = f32[64,64]{1,0:T(8,128)S(1)} all-gather(f32[8,64]{1,0:T(8,128)S(1)} %copy.85), channel_id=1, replica_groups=mesh['lat'=8,'lon'=4] {'lat'}, dimensions={0}, use_global_device_ids=true | all-gather | bytes 18432 | tf_op jit(solution)/shard_map/all_gather | solution.py:52
  (97 shorter events, 72.2 us)
Async XLA Ops:
  7.2 26.9 %copy-start.1 = (u32[32]{0:T(128)S(1)}, u32[32]{0:T(128)}, u32[]{:S(2)}) copy-start(u32[32]{0:T(128)} %constant.44) | copy-start | bytes 388
  7.2 56.4 %reduce-scatter.7.cloned.1.call-start = ((), (), s32[]{:S(2)}) async-start(), calls=%async_computation.3 | async-start | bytes 294912 | tf_op jit(solution)/shard_map/reduce_scatter | solution.py:50
  7.9 85.1 %copy-start = (f32[16,128]{1,0:T(8,128)S(1)}, f32[16,128]{1,0:T(8,128)}, u32[]{:S(2)}) copy-start(f32[16,128]{1,0:T(8,128)} %param.9) | copy-start | bytes 24580
  9.2 17.2 %collective-permute-start = (f32[64,1,128]{2,0,1:T(8,128)S(1)}, f32[64,1,128]{2,0,1:T(8,128)S(1)}, u32[]{:S(2)}, u32[]{:S(2)}) collective-permute-start(f32[64,1,128]{2,0,1:T(8,128)S(1)} %get-tuple-element.21), channel_id=1, source_target_pairs={{4,0},{8,4},{12,8},{16,12},{20,16},{24,20},{28,24},{5,1},{9,5},{13... | collective-permute-start | bytes 98312 | tf_op jit(solution)/shard_map/ppermute | solution.py:17
  10.5 16.0 %collective-permute-start.1 = (f32[64,1,128]{2,0,1:T(8,128)S(1)}, f32[64,1,128]{2,0,1:T(8,128)S(1)}, u32[]{:S(2)}, u32[]{:S(2)}) collective-permute-start(f32[64,1,128]{2,0,1:T(8,128)S(1)} %get-tuple-element.20), channel_id=1, source_target_pairs={{0,4},{4,8},{8,12},{12,16},{16,20},{20,24},{24,28},{1,5},{5,9},{9,... | collective-permute-start | bytes 98312 | tf_op jit(solution)/shard_map/ppermute | solution.py:14
  26.4 189.6 %reduce-scatter.9.cloned.1.call-start = ((), (), s32[]{:S(2)}) async-start(), calls=%async_computation.4 | async-start | bytes 294912 | tf_op jit(solution)/shard_map/reduce_scatter | solution.py:50
  26.9 8.4 %collective-permute-start.2 = (f32[64,18,1]{0,2,1:T(1,128)S(1)}, f32[64,18,1]{0,2,1:T(1,128)S(1)}, u32[]{:S(2)}, u32[]{:S(2)}) collective-permute-start(f32[64,18,1]{0,2,1:T(1,128)S(1)} %copy.43), channel_id=1, source_target_pairs={{1,0},{2,1},{3,2},{5,4},{6,5},{7,6},{9,8},{10,9},{11,10},{13,12},{... | collective-permute-start | bytes 13832 | tf_op jit(solution)/shard_map/ppermute | solution.py:17
  28.5 7.1 %collective-permute-start.3 = (f32[64,18,1]{0,2,1:T(1,128)S(1)}, f32[64,18,1]{0,2,1:T(1,128)S(1)}, u32[]{:S(2)}, u32[]{:S(2)}) collective-permute-start(f32[64,18,1]{0,2,1:T(1,128)S(1)} %copy.45), channel_id=1, source_target_pairs={{0,1},{1,2},{2,3},{4,5},{5,6},{6,7},{8,9},{9,10},{10,11},{12,13},{... | collective-permute-start | bytes 13832 | tf_op jit(solution)/shard_map/ppermute | solution.py:14
  164.2 16.5 %collective-permute-start.5 = (f32[64,1,128]{2,0,1:T(8,128)S(1)}, f32[64,1,128]{2,0,1:T(8,128)S(1)}, u32[]{:S(2)}, u32[]{:S(2)}) collective-permute-start(f32[64,1,128]{2,0,1:T(8,128)S(1)} %get-tuple-element.19), channel_id=1, source_target_pairs={{0,4},{4,8},{8,12},{12,16},{16,20},{20,24},{24,28},{1,5},{5,9},{9,... | collective-permute-start | bytes 98312 | tf_op jit(solution)/shard_map/ppermute | solution.py:14
  179.3 3.8 collective-permute-start.4
  180.6 188.2 %reduce-scatter.11.cloned.1.call-start = ((), (), s32[]{:S(2)}) async-start(), calls=%async_computation.5 | async-start | bytes 294912 | tf_op jit(solution)/shard_map/reduce_scatter | solution.py:50
  183.5 6.1 %collective-permute-start.6 = (f32[64,18,1]{0,2,1:T(1,128)S(1)}, f32[64,18,1]{0,2,1:T(1,128)S(1)}, u32[]{:S(2)}, u32[]{:S(2)}) collective-permute-start(f32[64,18,1]{0,2,1:T(1,128)S(1)} %copy.60), channel_id=1, source_target_pairs={{1,0},{2,1},{3,2},{5,4},{6,5},{7,6},{9,8},{10,9},{11,10},{13,12},{... | collective-permute-start | bytes 13832 | tf_op jit(solution)/shard_map/ppermute | solution.py:17
  185.1 5.9 %collective-permute-start.7 = (f32[64,18,1]{0,2,1:T(1,128)S(1)}, f32[64,18,1]{0,2,1:T(1,128)S(1)}, u32[]{:S(2)}, u32[]{:S(2)}) collective-permute-start(f32[64,18,1]{0,2,1:T(1,128)S(1)} %copy.62), channel_id=1, source_target_pairs={{0,1},{1,2},{2,3},{4,5},{5,6},{6,7},{8,9},{9,10},{10,11},{12,13},{... | collective-permute-start | bytes 13832 | tf_op jit(solution)/shard_map/ppermute | solution.py:14
  316.7 16.6 %collective-permute-start.9 = (f32[64,1,128]{2,0,1:T(8,128)S(1)}, f32[64,1,128]{2,0,1:T(8,128)S(1)}, u32[]{:S(2)}, u32[]{:S(2)}) collective-permute-start(f32[64,1,128]{2,0,1:T(8,128)S(1)} %get-tuple-element.17), channel_id=1, source_target_pairs={{0,4},{4,8},{8,12},{12,16},{16,20},{20,24},{24,28},{1,5},{5,9},{9,... | collective-permute-start | bytes 98312 | tf_op jit(solution)/shard_map/ppermute | solution.py:14
  331.7 3.8 collective-permute-start.8
  336.0 7.0 %collective-permute-start.10 = (f32[64,18,1]{0,2,1:T(1,128)S(1)}, f32[64,18,1]{0,2,1:T(1,128)S(1)}, u32[]{:S(2)}, u32[]{:S(2)}) collective-permute-start(f32[64,18,1]{0,2,1:T(1,128)S(1)} %copy.78), channel_id=1, source_target_pairs={{1,0},{2,1},{3,2},{5,4},{6,5},{7,6},{9,8},{10,9},{11,10},{13,12},{... | collective-permute-start | bytes 13832 | tf_op jit(solution)/shard_map/ppermute | solution.py:17
  337.6 5.9 %collective-permute-start.11 = (f32[64,18,1]{0,2,1:T(1,128)S(1)}, f32[64,18,1]{0,2,1:T(1,128)S(1)}, u32[]{:S(2)}, u32[]{:S(2)}) collective-permute-start(f32[64,18,1]{0,2,1:T(1,128)S(1)} %copy.80), channel_id=1, source_target_pairs={{0,1},{1,2},{2,3},{4,5},{5,6},{6,7},{8,9},{9,10},{10,11},{12,13},{... | collective-permute-start | bytes 13832 | tf_op jit(solution)/shard_map/ppermute | solution.py:14
Sparse Core Ops, SparseCore 0:
  26.5 37.0 reduce-scatter.6
  180.7 35.2 reduce-scatter.8
  333.4 35.2 reduce-scatter.10
where the time goes:
time: 473 us; the launch traced here: 464 us
  blocking collectives  231 us (49%)
  waiting for transfers between devices  83.4 us (18%)
  matrix products  70.9 us (15%)
  starting transfers between devices  30.3 us (6%)
  other arithmetic  26.2 us (6%)
  between operations  15.3 us (3%)
  local copies, waits for them, and re-layouts  6.75 us (1%)
    psum x6, blocking collectives, total_terms(): summed = lax.psum((shares[0],), 'lon')  106 us
    reduce_scatter x3, waiting for transfers between devices, total_terms(): lax.psum_scatter(term_tuple[0], 'lat', scatter_dimension=0, tiled=True)  77.5 us
    unnamed x3, blocking collectives  70.8 us
    all_gather x6, blocking collectives, total_terms(): return (lax.all_gather(summed[0], 'lat', axis=0, tiled=True),)  54.3 us
    dot_general x3, matrix products, project_points(): jnp.einsum('tab,kab->tk', snapshots, masked_field, precision=lax.Precisio...  38.5 us
    dot_general x3, matrix products, expand_points(): jnp.einsum('tab,tk->kab', snapshots, coeffs, precision=lax.Precision.HIGH...  29.4 us
    ppermute x6, starting transfers between devices, padded_2(): lax.ppermute(lax.slice_in_dim(block, block.shape[dim] - width, None, axis...  22.2 us
    another operation x6, other arithmetic, local(): factor = jnp.linalg.cholesky(moments / point_count)  13 us
  transfers between devices with their start and end apart: 15, of which 7 were waited for; matrix products, arithmetic and copies ran while one was open for 9% of the time, Pallas kernels for 0%

commit v1 on v0

v1 whole, which is shorter than its diff:
```python
import functools

import jax
import jax.numpy as jnp
from jax import lax
from jax.experimental import pallas as pl
from jax.experimental.pallas import tpu as pltpu
from jax.sharding import PartitionSpec as P

STEPS = 2
MESH = pl.DeviceIdType.MESH
F32 = jnp.float32
BF16 = jnp.bfloat16
NT = (((1,), (1,)), ((), ()))
NN = (((1,), (0,)), ((), ()))


def dot_low(a, b, dims):
    return lax.dot_general(a, b, dims, preferred_element_type=F32)


def dot_full(a, b, dims):
    return lax.dot_general(
        a, b, dims, precision=lax.Precision.HIGHEST, preferred_element_type=F32
    )


def split(x):
    high = x.astype(BF16)
    return high, (x - high.astype(F32)).astype(BF16)


def inverse_factor(gram):
    k = gram.shape[0]
    rows = lax.broadcasted_iota(jnp.int32, (k, k), 0)
    cols = lax.broadcasted_iota(jnp.int32, (k, k), 1)
    eye = jnp.where(rows == cols, 1.0, 0.0).astype(F32)
    work = jnp.concatenate([gram, eye], axis=1)
    blocks = [work[8 * i:8 * i + 8] for i in range(k // 8)]
    sub = lax.broadcasted_iota(jnp.int32, (8, 2 * k), 0)
    pivots = [jnp.zeros((8, 2 * k), F32) for _ in range(k // 8)]
    for j in range(k):
        own, at = j // 8, j % 8
        row = jnp.broadcast_to(blocks[own][at:at + 1, :], (8, 2 * k))
        columns = [
            jnp.broadcast_to(blocks[i][:, j:j + 1], (8, 2 * k)) for i in range(own, k // 8)
        ]
        pivot = jnp.broadcast_to(columns[0][at:at + 1, :], (8, 2 * k))
        pivots[own] = jnp.where(sub == at, pivot, pivots[own])
        scaled = row * (1.0 / pivot)
        for i in range(own, k // 8):
            column = columns[i - own]
            if i == own:
                column = jnp.where(sub > at, column, 0.0)
            blocks[i] = blocks[i] - column * scaled
    done = [blocks[i] * (1.0 / jnp.sqrt(pivots[i])) for i in range(k // 8)]
    return jnp.concatenate(done, axis=0)[:, k:]


def kernel(
    n, m, points, s_hbm, land_ref, pen_ref, v_hbm, out_hbm, ray_ref,
    s_full, s_high, s_mid, field0, field1, field2, lap_ref, out_buf, v_split, acc,
    cbuf, rs, zr, fin, gl, gz, edge, halo,
    s_sem, v_sem, o_sem, rs_s, rs_r, z_s, z_r, ag_s, ag_r, gl_s, gl_r, gz_s, gz_r, h_s, h_r,
):
    lat = lax.axis_index("lat")
    lon = lax.axis_index("lon")
    t_count, a_count, b_count = s_hbm.shape
    k = v_hbm.shape[0]
    fields = (field0, field1, field2)
    shard = cbuf.shape[1] // n
    inverse_points = 1.0 / points
    pending = []

    def part(a):
        return pl.ds(a * b_count, b_count)

    loads = []
    for a in range(a_count):
        loads.append(pltpu.make_async_copy(v_hbm.at[:, a, :], out_buf.at[:, part(a)], v_sem.at[a]))
    for a in range(a_count):
        loads.append(pltpu.make_async_copy(s_hbm.at[:, a, :], s_full.at[:, part(a)], s_sem.at[a]))
    for copy in loads:
        copy.start()

    barrier = pltpu.get_barrier_semaphore()
    for d in range(1, n):
        pl.semaphore_signal(
            barrier, inc=1, device_id=(lax.rem(lat + d, n), lon), device_id_type=MESH
        )
    for e in range(1, m):
        pl.semaphore_signal(
            barrier, inc=1, device_id=(lat, lax.rem(lon + e, m)), device_id_type=MESH
        )
    pl.semaphore_wait(barrier, n + m - 2)

    def send(src, dst, s_s, s_r, where):
        copy = pltpu.make_async_remote_copy(
            src_ref=src, dst_ref=dst, send_sem=s_s, recv_sem=s_r,
            device_id=where, device_id_type=MESH,
        )
        copy.start()
        pending.append(copy)
        return copy

    def to_lat(d):
        return (lax.rem(lat + d, n), lon)

    def to_lon(e):
        return (lat, lax.rem(lon + e, m))

    lane = lax.broadcasted_iota(jnp.int32, (k, b_count), 1)

    def mask_row(a):
        return land_ref[a:a + 1, :].astype(F32)

    def start_halo(r):
        x = fields[r]
        packed = jnp.zeros((k, b_count), F32)
        for a in range(a_count):
            block = x[:, a * b_count:(a + 1) * b_count]
            low = block if a == 0 else pltpu.roll(block, a, axis=1)
            high = pltpu.roll(block, a_count + a + 1, axis=1)
            packed = jnp.where(lane == a, low, packed)
            packed = jnp.where(lane == a_count + a, high, packed)
        edge[r] = packed
        return [
            send(x.at[:, part(a_count - 1)], halo.at[r, 0], h_s.at[r, 0], h_r.at[r, 0], to_lat(1)),
            send(x.at[:, part(0)], halo.at[r, 1], h_s.at[r, 1], h_r.at[r, 1], to_lat(n - 1)),
            send(edge.at[r], halo.at[r, 2], h_s.at[r, 2], h_r.at[r, 2], to_lon(1)),
            send(edge.at[r], halo.at[r, 3], h_s.at[r, 3], h_r.at[r, 3], to_lon(m - 1)),
        ]

    def laplacian(r, copies):
        for copy in copies:
            copy.wait_recv()
        x = fields[r]
        above = jnp.where(lat > 0, halo[r, 0], 0.0)
        below = jnp.where(lat < n - 1, halo[r, 1], 0.0)
        west = jnp.where(lon > 0, halo[r, 2], 0.0)
        east = jnp.where(lon < m - 1, halo[r, 3], 0.0)
        for a in range(a_count):
            block = x[:, a * b_count:(a + 1) * b_count]
            up = above if a == 0 else x[:, (a - 1) * b_count:a * b_count]
            down = below if a == a_count - 1 else x[:, (a + 1) * b_count:(a + 2) * b_count]
            left = jnp.where(
                lane == 0, pltpu.roll(west, b_count - a_count - a, axis=1),
                pltpu.roll(block, 1, axis=1),
            )
            right = jnp.where(
                lane == b_count - 1, pltpu.roll(east, b_count - 1 - a, axis=1),
                pltpu.roll(block, b_count - 1, axis=1),
            )
            total = (down + up + right + left) - 4.0 * block
            lap_ref[:, a * b_count:(a + 1) * b_count] = total * pen_ref[a:a + 1, :]

    def store_field(r, a, value):
        x = value * mask_row(a)
        high, mid = split(x)
        at = slice(a * b_count, (a + 1) * b_count)
        fields[r][:, at] = x
        v_split[:k, at] = high
        v_split[k:, at] = mid

    def store_coeffs(r, block, value):
        for w in range(value.shape[1] // b_count):
            row = (block * (value.shape[1] // b_count) + w) * k
            cbuf[r, row:row + k, :] = value[:, w * b_count:(w + 1) * b_count]

    def start_scatter(r):
        copies = []
        for d in range(1, n):
            there = lax.rem(lat + d, n)
            rows = pl.ds(pl.multiple_of(there * shard, shard), shard)
            copies.append(
                send(cbuf.at[r, rows], rs.at[r, d], rs_s.at[r, d], rs_r.at[r, d], to_lat(d))
            )
        return copies

    def own_rows():
        return pl.ds(pl.multiple_of(lat * shard, shard), shard)

    def finish_scatter(r, copies):
        total = cbuf[r, own_rows(), :]
        for d, copy in enumerate(copies):
            copy.wait_recv()
            total = total + rs[r, d + 1]
        zr[r, lon] = total
        return [
            send(zr.at[r, lon], zr.at[r, lon], z_s.at[r, e], z_r.at[r, e], to_lon(e))
            for e in range(1, m)
        ]

    def start_gather(r, copies):
        for copy in copies:
            copy.wait_recv()
        total = zr[r, 0]
        for e in range(1, m):
            total = total + zr[r, e]
        fin[r, own_rows(), :] = total
        return [
            send(fin.at[r, own_rows()], fin.at[r, own_rows()], ag_s.at[r, d], ag_r.at[r, d], to_lat(d))
            for d in range(1, n)
        ]

    def finish_gather(r, copies):
        for copy in copies:
            copy.wait_recv()
        return jnp.concatenate(
            [fin[r, i * k:(i + 1) * k, :] for i in range(t_count // b_count)], axis=1
        )

    def start_gram(r, value):
        gl[r, lat] = value
        return [
            send(gl.at[r, lat], gl.at[r, lat], gl_s.at[r, d], gl_r.at[r, d], to_lat(d))
            for d in range(1, n)
        ]

    def middle_gram(r, copies):
        for copy in copies:
            copy.wait_recv()
        total = gl[r, 0]
        for d in range(1, n):
            total = total + gl[r, d]
        gz[r, lon] = total
        return [
            send(gz.at[r, lon], gz.at[r, lon], gz_s.at[r, e], gz_r.at[r, e], to_lon(e))
            for e in range(1, m)
        ]

    def finish_gram(r, copies):
        for copy in copies:
            copy.wait_recv()
        total = gz[r, 0]
        for e in range(1, m):
            total = total + gz[r, e]
        return total

    def project(r):
        width = 2 * b_count
        for block in range(t_count // width):
            rows = slice(block * width, (block + 1) * width)
            both = dot_low(v_split[...], s_high[rows, :], NT)
            rest = dot_low(v_split[:k, :], s_mid[rows, :], NT)
            store_coeffs(r, block, both[:k] + (both[k:] + rest))

    def expand(r, coeffs):
        high, mid = split(coeffs)
        stacked = jnp.concatenate([high, mid], axis=0)
        width = 2 * b_count
        for block in range(a_count // 2):
            at = slice(block * width, (block + 1) * width)
            both = dot_low(stacked, s_high[:, at], NN)
            rest = dot_low(high, s_mid[:, at], NN)
            value = (both[:k] + (both[k:] + rest)) * inverse_points + lap_ref[:, at]
            store_field(r, 2 * block, value[:, :b_count])
            store_field(r, 2 * block + 1, value[:, b_count:])

    for a in range(a_count):
        loads[a].wait()
        store_field(0, a, out_buf[:, a * b_count:(a + 1) * b_count])
    halo_copies = start_halo(0)
    width = 2 * b_count
    for block in range(a_count // 2):
        at = slice(block * width, (block + 1) * width)
        loads[a_count + 2 * block].wait()
        loads[a_count + 2 * block + 1].wait()
        high, mid = split(s_full[:, at])
        s_high[:, at] = high
        s_mid[:, at] = mid
        both = dot_low(v_split[:, at], high, NT)
        rest = dot_low(v_split[:k, at], mid, NT)
        value = both[:k] + (both[k:] + rest)
        if block == 0:
            acc[...] = value
        else:
            acc[...] += value
    store_coeffs(0, 0, acc[...])
    copies = start_scatter(0)
    laplacian(0, halo_copies)
    copies = finish_scatter(0, copies)
    copies = start_gather(0, copies)
    expand(1, finish_gather(0, copies))

    halo_copies = start_halo(1)
    x = field1[...]
    gram = dot_full(x, x, NT) * inverse_points
    gram_copies = start_gram(0, jnp.concatenate([gram, gram], axis=1))
    project(1)
    copies = start_scatter(1)
    gram_copies = middle_gram(0, gram_copies)
    laplacian(1, halo_copies)
    copies = finish_scatter(1, copies)
    inverse = inverse_factor(finish_gram(0, gram_copies)[:, :k])
    copies = start_gather(1, copies)
    lap_ref[...] = dot_full(inverse, lap_ref[...], NN)
    expand(2, dot_full(inverse, finish_gather(1, copies), NN))

    halo_copies = start_halo(2)
    project(2)
    copies = start_scatter(2)
    laplacian(2, halo_copies)
    x = field2[...]
    gram = dot_full(x, x, NT) * inverse_points
    rough = dot_full(x, lap_ref[...], NT)
    gram_copies = start_gram(1, jnp.concatenate([gram, rough], axis=1))
    copies = finish_scatter(2, copies)
    gram_copies = middle_gram(1, gram_copies)
    copies = start_gather(2, copies)
    both = finish_gram(1, gram_copies)
    inverse = inverse_factor(both[:, :k])
    stores = []
    for a in range(a_count):
        at = slice(a * b_count, (a + 1) * b_count)
        out_buf[:, at] = dot_full(inverse, field2[:, at], NN)
        copy = pltpu.make_async_copy(out_buf.at[:, part(a)], out_hbm.at[:, a, :], o_sem.at[a])
        copy.start()
        stores.append(copy)
    coeffs = finish_gather(2, copies)
    middle = dot_full(coeffs, coeffs, NT) * inverse_points + both[:, k:]
    ray_ref[...] = dot_full(dot_full(inverse, middle, NN), inverse, NT) * inverse_points
    for copy in stores:
        copy.wait()
    for copy in pending:
        copy.wait_send()


def local(snapshots, land_sea, penalty, initial_basis):
    n, m = lax.axis_size("lat"), lax.axis_size("lon")
    t, a, b = snapshots.shape
    k = initial_basis.shape[0]
    points = float(a * b * n * m)
    p = a * b
    rows = t * k // b
    shard = rows // n
    sem = pltpu.SemaphoreType.DMA
    vmem = pltpu.VMEM
    any_spec = pl.BlockSpec(memory_space=pl.ANY)
    vmem_spec = pl.BlockSpec(memory_space=pltpu.VMEM)
    return pl.pallas_call(
        functools.partial(kernel, n, m, points),
        out_shape=(
            jax.ShapeDtypeStruct((k, a, b), F32),
            jax.ShapeDtypeStruct((k, k), F32),
        ),
        in_specs=[any_spec, vmem_spec, vmem_spec, any_spec],
        out_specs=(any_spec, vmem_spec),
        scratch_shapes=[
            vmem((t, p), F32), vmem((t, p), BF16), vmem((t, p), BF16),
            vmem((k, p), F32), vmem((k, p), F32), vmem((k, p), F32),
            vmem((k, p), F32), vmem((k, p), F32), vmem((2 * k, p), BF16), vmem((k, t), F32),
            vmem((3, rows, b), F32), vmem((3, n, shard, b), F32), vmem((3, m, shard, b), F32),
            vmem((3, rows, b), F32), vmem((2, n, k, b), F32), vmem((2, m, k, b), F32),
            vmem((3, k, b), F32), vmem((3, 4, k, b), F32),
            sem((a,)), sem((a,)), sem((a,)),
            sem((3, n)), sem((3, n)), sem((3, m)), sem((3, m)), sem((3, n)), sem((3, n)),
            sem((2, n)), sem((2, n)), sem((2, m)), sem((2, m)), sem((3, 4)), sem((3, 4)),
        ],
        compiler_params=pltpu.CompilerParams(
            collective_id=0, has_side_effects=True, vmem_limit_bytes=60 * 1024 * 1024
        ),
        name="power_steps",
    )(snapshots, land_sea, penalty, initial_basis)


def solution(mesh):
    in_specs = (P(None, "lat", "lon"), P("lat", "lon"), P("lat", "lon"), P(None, "lat", "lon"))
    out_specs = (P(None, "lat", "lon"), P())
    return jax.shard_map(local, mesh=mesh, in_specs=in_specs, out_specs=out_specs, check_vma=False)
```

time: 473 us -> 85.3 us (0.18); the launches traced: 464 us -> 85.1 us
  blocking collectives: 231 us -> 0 us
  waiting for transfers between devices: 83.4 us -> 0 us
  Pallas kernels: 0 us -> 81.2 us
  matrix products: 70.9 us -> 0 us
  starting transfers between devices: 30.3 us -> 0 us
  other arithmetic: 26.2 us -> 0 us
  between operations: 15.3 us -> 0.64 us
    psum x6 -> x0, blocking collectives: 106 us -> none  [total_terms(): summed = lax.psum((shares[0],), 'lon')]
    pallas_call x0 -> x1, Pallas kernels: none -> 81.2 us  [local(): pl.pallas_call(functools.partial(kernel, n, m, points), out_shape=(jax.Sh...]
    reduce_scatter x3 -> x0, waiting for transfers between devices: 77.5 us -> none  [total_terms(): lax.psum_scatter(term_tuple[0], 'lat', scatter_dimension=0, tiled=True)]
    unnamed x3 -> x0, blocking collectives: 70.8 us -> none
    dot_general x9 -> x0, matrix products: 69.6 us -> none  [the longest x3 38.5 us: project_points(): jnp.einsum('tab,kab->tk', snapshots, masked_field, precision=lax.Precisio...]
    all_gather x6 -> x0, blocking collectives: 54.3 us -> none  [total_terms(): return (lax.all_gather(summed[0], 'lat', axis=0, tiled=True),)]
    ppermute x12 -> x0, starting transfers between devices: 30.2 us -> none  [the longest x6 22.2 us: padded_2(): lax.ppermute(lax.slice_in_dim(block, block.shape[dim] - width, None, axis...]
    another operation x10 -> x0, other arithmetic: 24.1 us -> none  [the longest x6 13 us: local(): factor = jnp.linalg.cholesky(moments / point_count)]
  transfers between devices with their start and end apart: 15 -> 0, of which waited for: 7 -> 0; matrix products, arithmetic and copies ran while one was open for 9% -> 0% of each run, Pallas kernels for 0% -> 0%
where the time goes in v1:
time: 85.3 us; the launch traced here: 85.1 us
  Pallas kernels  81.2 us (95%)
  local copies, waits for them, and re-layouts  3.24 us (4%)
    pallas_call x1, Pallas kernels, local(): pl.pallas_call(functools.partial(kernel, n, m, points), out_shape=(jax.Sh...  81.2 us
    unnamed x2, local copies, waits for them, and re-layouts  3.24 us

profile of v1, /device:TPU:0, one launch (start us, length us, event | category | flops | bytes accessed | tf_op | source)
XLA Modules:
  0.0 85.1 jit_solution(910075508585507276)
XLA Ops:
  0.6 81.2 %power_steps.1 = (f32[64,16,128]{2,1,0:T(8,128)}, f32[64,64]{1,0:T(8,128)}) custom-call(f32[1024,16,128]{2,1,0:T(8,128)} %s_hbm.1, s32[16,128]{1,0:T(8,128)} %land_ref.1, f32[16,128]{1,0:T(8,128)} %pen_ref.1, f32[64,16,128]{2,1,0:T(8,128)} %v_hbm.1), custom_call_target="tpu_custom_call" | custom-call | tf_op jit(solution)/shard_map/power_steps/pallas_call | solution.py:341
  81.8 1.9 %copy.8 = f32[64,16,128]{2,1,0:T(8,128)} copy(f32[64,16,128]{2,1,0:T(8,128)} %get-tuple-element.4) | data formatting | bytes 1048576
  83.7 1.4 %copy.9 = f32[64,64]{1,0:T(8,128)} copy(f32[64,64]{1,0:T(8,128)} %get-tuple-element.5) | data formatting | bytes 32768

commit v2 on v1

--- a/solution.py
+++ b/solution.py
@@ -30,30 +30,80 @@
     return high, (x - high.astype(F32)).astype(BF16)
 
 
+def split3(x):
+    high = x.astype(BF16)
+    rest = x - high.astype(F32)
+    mid = rest.astype(BF16)
+    return jnp.concatenate([high, mid, (rest - mid.astype(F32)).astype(BF16)], axis=0)
+
+
+def fold_rows(x, k):
+    return x[:k] + (x[k:2 * k] + x[2 * k:])
+
+
+def products(left, right):
+    k = left.shape[0] // 3
+    x = fold_rows(dot_low(left, right, NT), k)
+    return x[:, :k] + (x[:, k:2 * k] + x[:, 2 * k:])
+
+
+def factor_parts(inverse):
+    k = inverse.shape[0]
+    parts = split3(inverse)
+    return jnp.concatenate([parts, parts, parts], axis=1)
+
+
+def times(parts, right):
+    return fold_rows(dot_low(parts, right, NN), parts.shape[0] // 3)
+
+
 def inverse_factor(gram):
     k = gram.shape[0]
+    panel = 4
     rows = lax.broadcasted_iota(jnp.int32, (k, k), 0)
     cols = lax.broadcasted_iota(jnp.int32, (k, k), 1)
     eye = jnp.where(rows == cols, 1.0, 0.0).astype(F32)
     work = jnp.concatenate([gram, eye], axis=1)
-    blocks = [work[8 * i:8 * i + 8] for i in range(k // 8)]
-    sub = lax.broadcasted_iota(jnp.int32, (8, 2 * k), 0)
-    pivots = [jnp.zeros((8, 2 * k), F32) for _ in range(k // 8)]
-    for j in range(k):
+    count = k // 8
+    shape = (8, 2 * k)
+    blocks = [work[8 * i:8 * i + 8] for i in range(count)]
+    sub = lax.broadcasted_iota(jnp.int32, shape, 0)
+    pivots = [jnp.zeros(shape, F32) for _ in range(count)]
+    for j in range(0, k, panel):
         own, at = j // 8, j % 8
-        row = jnp.broadcast_to(blocks[own][at:at + 1, :], (8, 2 * k))
-        columns = [
-            jnp.broadcast_to(blocks[i][:, j:j + 1], (8, 2 * k)) for i in range(own, k // 8)
-        ]
-        pivot = jnp.broadcast_to(columns[0][at:at + 1, :], (8, 2 * k))
-        pivots[own] = jnp.where(sub == at, pivot, pivots[own])
-        scaled = row * (1.0 / pivot)
-        for i in range(own, k // 8):
-            column = columns[i - own]
+        row = [jnp.broadcast_to(blocks[own][at + a:at + a + 1, :], shape) for a in range(panel)]
+        column = [
+            [jnp.broadcast_to(blocks[i][:, j + a:j + a + 1], shape) for i in range(own, count)]
+            for a in range(panel)
+        ]
+        corner = {
+            (b, a): jnp.broadcast_to(column[a][0][at + b:at + b + 1, :], shape)
+            for a in range(panel) for b in range(a, panel)
+        }
+        scaled = []
+        for a in range(panel):
+            pivot = corner[a, a]
+            pivots[own] = jnp.where(sub == at + a, pivot, pivots[own])
+            inverse = 1.0 / pivot
+            scaled.append(row[a] * inverse)
+            factor = {b: corner[b, a] * inverse for b in range(a + 1, panel)}
+            for b in range(a + 1, panel):
+                for c in range(b, panel):
+                    corner[c, b] = corner[c, b] - factor[b] * corner[c, a]
+            for b in range(a + 1, panel):
+                row[b] = row[b] - factor[b] * row[a]
+                column[b] = [y - factor[b] * x for x, y in zip(column[a], column[b])]
+        for i in range(own, count):
+            change = column[0][i - own] * scaled[0]
+            for a in range(1, panel):
+                change = change + column[a][i - own] * scaled[a]
+            value = blocks[i] - change
             if i == own:
-                column = jnp.where(sub > at, column, 0.0)
-            blocks[i] = blocks[i] - column * scaled
-    done = [blocks[i] * (1.0 / jnp.sqrt(pivots[i])) for i in range(k // 8)]
+                value = jnp.where(sub >= at + panel, value, blocks[i])
+                for a in range(panel):
+                    value = jnp.where(sub == at + a, row[a], value)
+            blocks[i] = value
+    done = [blocks[i] * (1.0 / jnp.sqrt(pivots[i])) for i in range(count)]
     return jnp.concatenate(done, axis=0)[:, k:]
 
 
@@ -156,11 +206,9 @@
 
     def store_field(r, a, value):
         x = value * mask_row(a)
-        high, mid = split(x)
         at = slice(a * b_count, (a + 1) * b_count)
         fields[r][:, at] = x
-        v_split[:k, at] = high
-        v_split[k:, at] = mid
+        v_split[:, at] = split3(x)
 
     def store_coeffs(r, block, value):
         for w in range(value.shape[1] // b_count):
@@ -241,7 +289,7 @@
         width = 2 * b_count
         for block in range(t_count // width):
             rows = slice(block * width, (block + 1) * width)
-            both = dot_low(v_split[...], s_high[rows, :], NT)
+            both = dot_low(v_split[:2 * k, :], s_high[rows, :], NT)
             rest = dot_low(v_split[:k, :], s_mid[rows, :], NT)
             store_coeffs(r, block, both[:k] + (both[k:] + rest))
 
@@ -269,7 +317,7 @@
         high, mid = split(s_full[:, at])
         s_high[:, at] = high
         s_mid[:, at] = mid
-        both = dot_low(v_split[:, at], high, NT)
+        both = dot_low(v_split[:2 * k, at], high, NT)
         rest = dot_low(v_split[:k, at], mid, NT)
         value = both[:k] + (both[k:] + rest)
         if block == 0:
@@ -284,41 +332,41 @@
     expand(1, finish_gather(0, copies))
 
     halo_copies = start_halo(1)
-    x = field1[...]
-    gram = dot_full(x, x, NT) * inverse_points
+    gram = products(v_split[...], v_split[...]) * inverse_points
     gram_copies = start_gram(0, jnp.concatenate([gram, gram], axis=1))
     project(1)
     copies = start_scatter(1)
     gram_copies = middle_gram(0, gram_copies)
     laplacian(1, halo_copies)
     copies = finish_scatter(1, copies)
-    inverse = inverse_factor(finish_gram(0, gram_copies)[:, :k])
+    parts = factor_parts(inverse_factor(finish_gram(0, gram_copies)[:, :k]))
     copies = start_gather(1, copies)
-    lap_ref[...] = dot_full(inverse, lap_ref[...], NN)
-    expand(2, dot_full(inverse, finish_gather(1, copies), NN))
+    lap_ref[...] = times(parts, split3(lap_ref[...]))
+    expand(2, times(parts, split3(finish_gather(1, copies))))
 
     halo_copies = start_halo(2)
     project(2)
     copies = start_scatter(2)
     laplacian(2, halo_copies)
-    x = field2[...]
-    gram = dot_full(x, x, NT) * inverse_points
-    rough = dot_full(x, lap_ref[...], NT)
+    gram = products(v_split[...], v_split[...]) * inverse_points
+    rough = products(v_split[...], split3(lap_ref[...]))
     gram_copies = start_gram(1, jnp.concatenate([gram, rough], axis=1))
     copies = finish_scatter(2, copies)
     gram_copies = middle_gram(1, gram_copies)
     copies = start_gather(2, copies)
     both = finish_gram(1, gram_copies)
     inverse = inverse_factor(both[:, :k])
+    parts = factor_parts(inverse)
     stores = []
     for a in range(a_count):
         at = slice(a * b_count, (a + 1) * b_count)
-        out_buf[:, at] = dot_full(inverse, field2[:, at], NN)
+        out_buf[:, at] = times(parts, v_split[:, at])
         copy = pltpu.make_async_copy(out_buf.at[:, part(a)], out_hbm.at[:, a, :], o_sem.at[a])
         copy.start()
         stores.append(copy)
     coeffs = finish_gather(2, copies)
-    middle = dot_full(coeffs, coeffs, NT) * inverse_points + both[:, k:]
+    coeffs = split3(coeffs)
+    middle = products(coeffs, coeffs) * inverse_points + both[:, k:]
     ray_ref[...] = dot_full(dot_full(inverse, middle, NN), inverse, NT) * inverse_points
     for copy in stores:
         copy.wait()
@@ -349,7 +397,7 @@
         scratch_shapes=[
             vmem((t, p), F32), vmem((t, p), BF16), vmem((t, p), BF16),
             vmem((k, p), F32), vmem((k, p), F32), vmem((k, p), F32),
-            vmem((k, p), F32), vmem((k, p), F32), vmem((2 * k, p), BF16), vmem((k, t), F32),
+            vmem((k, p), F32), vmem((k, p), F32), vmem((3 * k, p), BF16), vmem((k, t), F32),
             vmem((3, rows, b), F32), vmem((3, n, shard, b), F32), vmem((3, m, shard, b), F32),
             vmem((3, rows, b), F32), vmem((2, n, k, b), F32), vmem((2, m, k, b), F32),
             vmem((3, k, b), F32), vmem((3, 4, k, b), F32),

time: 85.3 us -> 73.7 us (0.86)
  Pallas kernels: 81.2 us -> 69.6 us
    pallas_call x1, Pallas kernels: 81.2 us -> 69.6 us  [local(): pl.pallas_call(functools.partial(kernel, n, m, points), out_shape=(jax.Sh...]
where the time goes in v2:
time: 73.7 us; the launch traced here: 73.5 us
  Pallas kernels  69.6 us (94%)
  local copies, waits for them, and re-layouts  3.24 us (4%)
    pallas_call x1, Pallas kernels, local(): pl.pallas_call(functools.partial(kernel, n, m, points), out_shape=(jax.Sh...  69.6 us
    unnamed x2, local copies, waits for them, and re-layouts  3.24 us

profile of v2, /device:TPU:0, one launch (start us, length us, event | category | flops | bytes accessed | tf_op | source)
XLA Modules:
  0.0 73.5 jit_solution(10788207939262459356)
XLA Ops:
  0.6 69.6 %power_steps.1 = (f32[64,16,128]{2,1,0:T(8,128)}, f32[64,64]{1,0:T(8,128)}) custom-call(f32[1024,16,128]{2,1,0:T(8,128)} %s_hbm.1, s32[16,128]{1,0:T(8,128)} %land_ref.1, f32[16,128]{1,0:T(8,128)} %pen_ref.1, f32[64,16,128]{2,1,0:T(8,128)} %v_hbm.1), custom_call_target="tpu_custom_call" | custom-call | tf_op jit(solution)/shard_map/power_steps/pallas_call | solution.py:389
  70.2 1.9 %copy.8 = f32[64,16,128]{2,1,0:T(8,128)} copy(f32[64,16,128]{2,1,0:T(8,128)} %get-tuple-element.4) | data formatting | bytes 1048576
  72.1 1.4 %copy.9 = f32[64,64]{1,0:T(8,128)} copy(f32[64,64]{1,0:T(8,128)} %get-tuple-element.5) | data formatting | bytes 32768

commit v3 on v2

--- a/solution.py
+++ b/solution.py
@@ -119,6 +119,7 @@
     k = v_hbm.shape[0]
     fields = (field0, field1, field2)
     shard = cbuf.shape[1] // n
+    half = shard // 2
     inverse_points = 1.0 / points
     pending = []
 
@@ -215,41 +216,57 @@
             row = (block * (value.shape[1] // b_count) + w) * k
             cbuf[r, row:row + k, :] = value[:, w * b_count:(w + 1) * b_count]
 
+    def band_rows(owner, h):
+        return pl.ds(pl.multiple_of(owner * shard + h * half, half), half)
+
     def start_scatter(r):
         copies = []
-        for d in range(1, n):
-            there = lax.rem(lat + d, n)
-            rows = pl.ds(pl.multiple_of(there * shard, shard), shard)
-            copies.append(
-                send(cbuf.at[r, rows], rs.at[r, d], rs_s.at[r, d], rs_r.at[r, d], to_lat(d))
+        for h in range(2):
+            into = pl.ds(h * half, half)
+            copies.append([
+                send(
+                    cbuf.at[r, band_rows(lax.rem(lat + d, n), h)], rs.at[r, d, into],
+                    rs_s.at[r, h, d], rs_r.at[r, h, d], to_lat(d),
+                )
+                for d in range(1, n)
+            ])
+        return copies
+
+    def finish_scatter(r, copies):
+        sends = []
+        for h in range(2):
+            into = pl.ds(h * half, half)
+            total = cbuf[r, band_rows(lat, h), :]
+            for d, copy in enumerate(copies[h]):
+                copy.wait_recv()
+                total = total + rs[r, d + 1, h * half:(h + 1) * half, :]
+            zr[r, lon, h * half:(h + 1) * half, :] = total
+            sends.append([
+                send(
+                    zr.at[r, lon, into], zr.at[r, lon, into],
+                    z_s.at[r, h, e], z_r.at[r, h, e], to_lon(e),
+                )
+                for e in range(1, m)
+            ])
+        return sends
+
+    def start_gather(r, copies):
+        sends = []
+        for h in range(2):
+            for copy in copies[h]:
+                copy.wait_recv()
+            total = zr[r, 0, h * half:(h + 1) * half, :]
+            for e in range(1, m):
+                total = total + zr[r, e, h * half:(h + 1) * half, :]
+            fin[r, band_rows(lat, h), :] = total
+            sends.extend(
+                send(
+                    fin.at[r, band_rows(lat, h)], fin.at[r, band_rows(lat, h)],
+                    ag_s.at[r, h, d], ag_r.at[r, h, d], to_lat(d),
+                )
+                for d in range(1, n)
             )
-        return copies
-
-    def own_rows():
-        return pl.ds(pl.multiple_of(lat * shard, shard), shard)
-
-    def finish_scatter(r, copies):
-        total = cbuf[r, own_rows(), :]
-        for d, copy in enumerate(copies):
-            copy.wait_recv()
-            total = total + rs[r, d + 1]
-        zr[r, lon] = total
-        return [
-            send(zr.at[r, lon], zr.at[r, lon], z_s.at[r, e], z_r.at[r, e], to_lon(e))
-            for e in range(1, m)
-        ]
-
-    def start_gather(r, copies):
-        for copy in copies:
-            copy.wait_recv()
-        total = zr[r, 0]
-        for e in range(1, m):
-            total = total + zr[r, e]
-        fin[r, own_rows(), :] = total
-        return [
-            send(fin.at[r, own_rows()], fin.at[r, own_rows()], ag_s.at[r, d], ag_r.at[r, d], to_lat(d))
-            for d in range(1, n)
-        ]
+        return sends
 
     def finish_gather(r, copies):
         for copy in copies:
@@ -402,7 +419,7 @@
             vmem((3, rows, b), F32), vmem((2, n, k, b), F32), vmem((2, m, k, b), F32),
             vmem((3, k, b), F32), vmem((3, 4, k, b), F32),
             sem((a,)), sem((a,)), sem((a,)),
-            sem((3, n)), sem((3, n)), sem((3, m)), sem((3, m)), sem((3, n)), sem((3, n)),
+            sem((3, 2, n)), sem((3, 2, n)), sem((3, 2, m)), sem((3, 2, m)), sem((3, 2, n)), sem((3, 2, n)),
             sem((2, n)), sem((2, n)), sem((2, m)), sem((2, m)), sem((3, 4)), sem((3, 4)),
         ],
         compiler_params=pltpu.CompilerParams(

time: 73.7 us -> 74.4 us (level)
  no operation moved by 1% of the time
where the time goes in v3:
time: 74.4 us; the launch traced here: 74.1 us
  Pallas kernels  70.2 us (94%)
  local copies, waits for them, and re-layouts  3.24 us (4%)
    pallas_call x1, Pallas kernels, local(): pl.pallas_call(functools.partial(kernel, n, m, points), out_shape=(jax.Sh...  70.2 us
    unnamed x2, local copies, waits for them, and re-layouts  3.24 us

profile of v3, /device:TPU:0, one launch (start us, length us, event | category | flops | bytes accessed | tf_op | source)
XLA Modules:
  0.0 74.1 jit_solution(6281249528158951537)
XLA Ops:
  0.6 70.2 %power_steps.1 = (f32[64,16,128]{2,1,0:T(8,128)}, f32[64,64]{1,0:T(8,128)}) custom-call(f32[1024,16,128]{2,1,0:T(8,128)} %s_hbm.1, s32[16,128]{1,0:T(8,128)} %land_ref.1, f32[16,128]{1,0:T(8,128)} %pen_ref.1, f32[64,16,128]{2,1,0:T(8,128)} %v_hbm.1), custom_call_target="tpu_custom_call" | custom-call | tf_op jit(solution)/shard_map/power_steps/pallas_call | solution.py:406
  70.9 1.9 %copy.8 = f32[64,16,128]{2,1,0:T(8,128)} copy(f32[64,16,128]{2,1,0:T(8,128)} %get-tuple-element.4) | data formatting | bytes 1048576
  72.7 1.4 %copy.9 = f32[64,64]{1,0:T(8,128)} copy(f32[64,64]{1,0:T(8,128)} %get-tuple-element.5) | data formatting | bytes 32768
